TPU v7x, 128 devices: a whole 4x4x4 slice. The times are simulated.
128 devices in a mesh: blk: 4 (over x_lo, core), shard: 32 (over x_hi, y, z).
Axes of the slice: x: 4 (x_hi: 2, x_lo: 2; x = x_hi * 2 + x_lo), y: 4, z: 4, core: 2. Of those that a mesh axis runs over, the one named last changes fastest.
Arguments:
- item_features: bfloat16 [131072, 1024], P('shard'), may hold values from -6 to 6
- tower_weight: bfloat16 [1024, 512], replicated, may hold values from -0.1875 to 0.1875
- gate_in: bfloat16 [64, 128], replicated, may hold values from -0.75 to 0.75
- gate_in_bias: bfloat16 [128], replicated, may hold values from -4 to 4
- gate_out: bfloat16 [128, 64], replicated, may hold values from -0.5 to 0.5
- gate_out_bias: bfloat16 [64], replicated, may hold values from -4 to 4
- user_table: bfloat16 [16384, 512], P(('blk', 'shard')), may hold values from -6 to 6
- user_ids: int32 [512], P(('blk', 'shard')), may hold values from 0 to 127
- positive_item: int32 [512, 16], P(('blk', 'shard')), may hold values from 0 to 7167
- listed_owner: int32 [1792, 1], P(('blk', 'shard')), may hold values from 0 to 31; in each aligned block of 14 rows (0 to 13, 14 to 27, ...) at most 2 rows name the same one
- listed_slot: int32 [1792], P(('blk', 'shard')), may hold values from 0 to 31
Outputs:
- tower_gradient: float32 [1024, 512], P('shard')
- user_gradient: float32 [16384, 512], P(('blk', 'shard'))
Inputs may be any that keep to these rules, and one draw needn't show every extreme that they name: `listed_owner`: at most 2 of the 14 listings of one trainer name the same owner. `user_ids`: A row of the trainer's own 128 rows of user_table. `positive_item`: A position among the rows of the user's circle.
All inputs are finite; a program needn't handle non-finite values.
Results may differ from a plain program's by a relative error of at most 0.0055.
Values may be sent and summed in bfloat16 or wider, within the bound.
No kernel may reach another device: no remote copies, remote signals or barrier semaphores. Data moves between devices by JAX's collectives and lax.ppermute only.
A program may use at most 128 MiB of HBM per device.

v0:
```python
import math
import jax
import jax.numpy as jnp
from jax import lax
from jax.sharding import PartitionSpec as P

K = 8
H = 64
BLK = 128
CAP = 2
OWN = 32
USERS = 4
UTAB = 128
E = 512


def from_behind(x, axis, by):
    peers = lax.axis_size(axis)
    return lax.ppermute(x, axis, [(i, (i + by) % peers) for i in range(peers)])


def pair_terms(user_rows, item_rows, targets, gate_in, gate_in_bias, gate_out, gate_out_bias):
    count_users = user_rows.shape[0]
    count_items = item_rows.shape[0]
    scaling = 1.0 / math.sqrt(H)
    user_parts = user_rows.reshape(count_users * K, H)
    item_parts = item_rows.reshape(count_items, K, H)
    logits = (
        jnp.einsum("xh,ibh->xbi", user_parts, item_parts, preferred_element_type=jnp.float32)
        * scaling
    )
    logits = logits.reshape(count_users, K * K, count_items)
    gate_input = logits.astype(jnp.bfloat16)
    hidden_pre = jnp.einsum("pg,upi->ugi", gate_in, gate_input, preferred_element_type=jnp.float32)
    hidden_pre = hidden_pre + gate_in_bias.astype(jnp.float32)[None, :, None]
    hidden = jax.nn.silu(hidden_pre).astype(jnp.bfloat16)
    gate_logit = jnp.einsum("gp,ugi->upi", gate_out, hidden, preferred_element_type=jnp.float32)
    gate_logit = gate_logit + gate_out_bias.astype(jnp.float32)[None, :, None]
    exp_terms = jnp.exp(gate_logit)
    mixture = exp_terms / jnp.sum(exp_terms, axis=1, keepdims=True)
    scores = jnp.sum(mixture * logits, axis=1)
    score_grad = jax.nn.sigmoid(scores) - targets
    weighted = score_grad[:, None, :] * mixture
    logit_grad = (weighted * (logits - scores[:, None, :])).astype(jnp.bfloat16)
    gate_sig = jax.nn.sigmoid(hidden_pre)
    hidden_grad = jnp.einsum(
        "gp,upi->ugi", gate_out, logit_grad, preferred_element_type=jnp.float32
    )
    hidden_grad = (hidden_grad * gate_sig * (1.0 + hidden_pre * (1.0 - gate_sig))).astype(
        jnp.bfloat16
    )
    pair_grad = weighted + jnp.einsum(
        "pg,ugi->upi", gate_in, hidden_grad, preferred_element_type=jnp.float32
    )
    pair_grad = pair_grad.astype(jnp.bfloat16).reshape(count_users * K, K, count_items)
    user_delta = jnp.einsum(
        "xbi,ibh->xh", pair_grad, item_parts, preferred_element_type=jnp.float32
    )
    item_delta = jnp.einsum(
        "xbi,xh->ibh", pair_grad, user_parts, preferred_element_type=jnp.float32
    )
    return (
        user_delta.reshape(count_users, K * H) * scaling,
        item_delta.reshape(count_items, K * H) * scaling,
    )


def match_targets(positives, first_column, count):
    columns = first_column + jnp.arange(count, dtype=jnp.int32)
    return jnp.any(positives[:, :, None] == columns[None, None, :], axis=1).astype(jnp.float32)


def split_product(left_bf16, right_f32):
    upper = right_f32.astype(jnp.bfloat16)
    lower = (right_f32 - upper.astype(jnp.float32)).astype(jnp.bfloat16)
    dims = (((0,), (0,)), ((), ()))
    first = lax.dot_general(left_bf16, upper, dims, preferred_element_type=jnp.float32)
    second = lax.dot_general(left_bf16, lower, dims, preferred_element_type=jnp.float32)
    return first + second


def shards(
    item_features,
    tower_weight,
    gate_in,
    gate_in_bias,
    gate_out,
    gate_out_bias,
    user_table,
    user_ids,
    positive_item,
    listed_owner,
    listed_slot,
):
    block_groups = lax.axis_size("blk")
    owner_count = lax.axis_size("shard")
    group_index = lax.axis_index("blk")
    listings = listed_slot.shape[0]
    circle_part = listings * BLK
    owner_ids = listed_owner[:, 0]
    listing_order = jnp.arange(listings, dtype=jnp.int32)
    same_owner = owner_ids[:, None] == owner_ids[None, :]
    earlier = listing_order[None, :] < listing_order[:, None]
    rank_within = jnp.sum(jnp.logical_and(same_owner, earlier), axis=1)
    owner_match = owner_ids[:, None] == jnp.arange(owner_count, dtype=jnp.int32)[None, :]
    rank_match = rank_within[:, None] == jnp.arange(CAP, dtype=jnp.int32)[None, :]
    placement = jnp.logical_and(owner_match[:, :, None], rank_match[:, None, :])
    wanted = jnp.sum(jnp.where(placement, listed_slot[:, None, None] + 1, 0), axis=0) - 1
    asked_slots = lax.all_to_all(wanted, "shard", split_axis=0, concat_axis=0, tiled=True)
    slot_pick = jnp.clip(asked_slots, 0, OWN - 1).reshape(-1)
    slot_of = owner_ids * CAP + rank_within
    own_vectors = jnp.dot(item_features, tower_weight, preferred_element_type=jnp.float32).astype(
        jnp.bfloat16
    )
    own_vectors = own_vectors.reshape(OWN, BLK, E)
    outgoing = jnp.take(own_vectors, slot_pick, axis=0).reshape(owner_count, CAP, BLK, E)
    arrived = lax.all_to_all(outgoing, "shard", split_axis=0, concat_axis=0, tiled=True).reshape(
        owner_count * CAP, BLK, E
    )
    listed = jnp.take(arrived, slot_of, axis=0).reshape(circle_part, E)
    row_match = user_ids[:, None] == jnp.arange(UTAB, dtype=jnp.int32)[None, :]
    user_rows = jnp.dot(
        row_match.astype(jnp.bfloat16), user_table, preferred_element_type=jnp.float32
    ).astype(jnp.bfloat16)
    moving = listed
    accumulator = jnp.zeros((circle_part, E), jnp.float32)
    user_delta = jnp.zeros((USERS, E), jnp.float32)
    for rotation in range(block_groups):
        anchor = jnp.mod(group_index - rotation, block_groups)
        targets = match_targets(positive_item, anchor * circle_part, circle_part)
        user_term, item_term = pair_terms(
            user_rows, moving, targets, gate_in, gate_in_bias, gate_out, gate_out_bias
        )
        user_delta = user_delta + user_term
        accumulator = from_behind(accumulator + item_term, "blk", 1)
        if rotation + 1 < block_groups:
            moving = from_behind(moving, "blk", 1)
    listing_grads = accumulator.astype(jnp.bfloat16)
    returning = jnp.zeros((owner_count * CAP, BLK, E), jnp.bfloat16)
    returning = returning.at[slot_of].set(listing_grads.reshape(listings, BLK, E))
    returned = lax.all_to_all(
        returning.reshape(owner_count, CAP, BLK, E),
        "shard",
        split_axis=0,
        concat_axis=0,
        tiled=True,
    )
    returned = returned.reshape(owner_count * CAP, BLK * E)
    slot_hot = (
        asked_slots.reshape(-1)[None, :] == jnp.arange(OWN, dtype=jnp.int32)[:, None]
    ).astype(jnp.bfloat16)
    summed = jnp.dot(slot_hot, returned, preferred_element_type=jnp.float32).reshape(OWN * BLK, E)
    partial_value = split_product(item_features, summed)
    tower_part = lax.psum_scatter(partial_value, "shard", scatter_dimension=0, tiled=True)
    tower_gradient = lax.psum(tower_part, "blk")
    user_gradient = split_product(row_match.astype(jnp.bfloat16), user_delta)
    return (tower_gradient, user_gradient)


def solution(mesh):
    return jax.shard_map(
        shards,
        mesh=mesh,
        in_specs=(
            P("shard", None),
            P(),
            P(),
            P(),
            P(),
            P(),
            P(("blk", "shard"), None),
            P(("blk", "shard")),
            P(("blk", "shard"), None),
            P(("blk", "shard"), None),
            P(("blk", "shard")),
        ),
        out_specs=(P("shard", None), P(("blk", "shard"), None)),
        check_vma=False,
    )
```

profile of v0, /device:TPU:1, one launch (start us, length us, event | category | flops | bytes accessed | tf_op | source)
XLA Modules:
  0.0 870.0 jit_solution(14057466203700951652)
XLA Ops:
  10.4 11.3 %all-to-all-start = ((s32[32,1,2]{2,1,0:T(1,128)}), s32[32,1,2]{2,1,0:T(1,128)S(1)}, u32[]{:S(2)}, u32[]{:S(2)}) async-start(s32[32,1,2]{2,1,0:T(1,128)} %copy.99), calls=%async_computation | async-start | bytes 32768 | tf_op jit(solution)/shard_map/all_to_all | solution.py:109
  21.8 9.5 %convolution_convert_fusion = bf16[4096,512]{1,0:T(8,128)(2,1)} fusion(bf16[4096,1024]{1,0:T(8,128)(2,1)} %param.11, bf16[1024,512]{1,0:T(8,128)(2,1)S(1)} %copy-done), kind=kOutput, calls=%fused_computation.9 | convolution fusion | flops 4297064448 | bytes 13631488 | tf_op jit(solution)/shard_map/dot_general | solution.py:112
  32.8 7.5 gather_fusion
  40.3 7.5 broadcast_select_fusion
  47.8 9.6 %all-to-all-start.1 = ((bf16[32,2,128,512]{3,2,1,0:T(8,128)(2,1)}), bf16[32,2,128,512]{3,2,1,0:T(8,128)(2,1)}, u32[]{:S(2)}, u32[]{:S(2)}) async-start(bf16[32,2,128,512]{3,2,1,0:T(8,128)(2,1)} %broadcast_select_fusion), calls=%async_computation.1 | async-start | bytes 16777216 | tf_op jit(solution)/shard_map/all_to_all | solution.py:117
  58.4 108.7 %all-to-all-done.1 = bf16[32,2,128,512]{3,2,1,0:T(8,128)(2,1)} async-done(((bf16[32,2,128,512]{3,2,1,0:T(8,128)(2,1)}), bf16[32,2,128,512]{3,2,1,0:T(8,128)(2,1)}, u32[]{:S(2)}, u32[]{:S(2)}) %all-to-all-start.1) | async-done | bytes 8388640 | tf_op jit(solution)/shard_map/all_to_all | solution.py:117
  174.6 14.0 %collective-permute-start.1 = (bf16[1792,512]{1,0:T(8,128)(2,1)}, bf16[1792,512]{1,0:T(8,128)(2,1)}, u32[]{:S(2)}, u32[]{:S(2)}) collective-permute-start(bf16[1792,512]{1,0:T(8,128)(2,1)} %bitcast_select_fusion), channel_id=1, source_target_pairs={{0,32},{32,64},{64,96},{96,0},{1,33},{33,65},{65,97},{97,1},{2,34}... | collective-permute-start | bytes 5505032 | tf_op jit(solution)/shard_map/ppermute | solution.py:19
  249.8 5.5 copy.113
  271.1 40.2 %collective-permute-done.5 = bf16[1792,512]{1,0:T(8,128)(2,1)} collective-permute-done((bf16[1792,512]{1,0:T(8,128)(2,1)}, bf16[1792,512]{1,0:T(8,128)(2,1)}, u32[]{:S(2)}, u32[]{:S(2)}) %collective-permute-start.5) | collective-permute-done | bytes 1835040 | tf_op jit(solution)/shard_map/ppermute | solution.py:19
  334.5 6.1 fusion.55
  349.4 15.8 %collective-permute-done.2 = f32[1792,512]{1,0:T(8,128)} collective-permute-done((f32[1792,512]{1,0:T(8,128)}, f32[1792,512]{1,0:T(8,128)}, u32[]{:S(2)}, u32[]{:S(2)}) %collective-permute-start.2) | collective-permute-done | bytes 3670048 | tf_op jit(solution)/shard_map/ppermute | solution.py:19
  365.3 5.9 add.319
  377.6 5.2 fusion.56
  390.5 23.4 %collective-permute-done.4 = f32[1792,512]{1,0:T(8,128)} collective-permute-done((f32[1792,512]{1,0:T(8,128)}, f32[1792,512]{1,0:T(8,128)}, u32[]{:S(2)}, u32[]{:S(2)}) %collective-permute-start.4) | collective-permute-done | bytes 3670048 | tf_op jit(solution)/shard_map/ppermute | solution.py:19
  420.4 20.2 %collective-permute-done.6 = bf16[1792,512]{1,0:T(8,128)(2,1)S(1)} collective-permute-done((bf16[1792,512]{1,0:T(8,128)(2,1)S(1)}, bf16[1792,512]{1,0:T(8,128)(2,1)S(1)}, u32[]{:S(2)}, u32[]{:S(2)}) %collective-permute-start.6) | collective-permute-done | bytes 1835040 | tf_op jit(solution)/shard_map/ppermute | solution.py:19
  450.0 8.0 all-to-all-start.2
  458.2 123.4 %all-to-all-done.2 = bf16[32,2,128,512]{3,2,1,0:T(8,128)(2,1)} async-done(((bf16[32,2,128,512]{3,2,1,0:T(8,128)(2,1)}), bf16[32,2,128,512]{3,2,1,0:T(8,128)(2,1)}, u32[]{:S(2)}, u32[]{:S(2)}) %all-to-all-start.2) | async-done | bytes 8388640 | tf_op jit(solution)/shard_map/all_to_all | solution.py:141
  581.5 11.7 %copy.142 = bf16[8,8,128,512]{3,1,2,0:T(8,128)(2,1)} copy(bf16[8,8,128,512]{3,2,1,0:T(8,128)(2,1)} %bitcast.67) | data formatting | bytes 16777216
  593.3 7.8 fusion.121
  601.1 7.5 reshape.288
  608.6 10.8 %fusion.4 = f32[512,1024]{1,0:T(8,128)S(1)} fusion(bf16[4096,1024]{1,0:T(8,128)(2,1)} %param.11, f32[4096,512]{1,0:T(8,128)} %reshape.288), kind=kOutput, calls=%fused_computation.10 | convolution fusion | flops 4303355904 | bytes 18874368 | tf_op jit(solution)/shard_map/dot_general | solution.py:78
  619.3 7.1 add_bitcast_fusion
  641.3 162.8 %reduce-scatter.4.cloned.1.call-done = f32[32,512]{1,0:T(8,128)} async-done(((f32[1024,512]{1,0:T(8,128)}), f32[32,512]{1,0:T(8,128)}) %reduce-scatter.4.cloned.1.call-update) | async-done | bytes 65552
  806.8 54.4 %all-reduce.2.cloned.1.call-done = f32[32,512]{0,1:T(8,128)} async-done(((f32[32,512]{0,1:T(8,128)}), f32[32,512]{0,1:T(8,128)}) %all-reduce.2.cloned.1.call-update) | async-done | bytes 65552 | tf_op jit(solution)/shard_map/psum | solution.py:155
  (179 shorter events, 171.1 us)
Async XLA Ops:
  7.2 14.6 %copy-start = (bf16[1024,512]{1,0:T(8,128)(2,1)S(1)}, bf16[1024,512]{1,0:T(8,128)(2,1)}, u32[]{:S(2)}) copy-start(bf16[1024,512]{1,0:T(8,128)(2,1)} %param.12) | copy-start | bytes 3145732
  10.4 20.8 %all-to-all-start = ((s32[32,1,2]{2,1,0:T(1,128)}), s32[32,1,2]{2,1,0:T(1,128)S(1)}, u32[]{:S(2)}, u32[]{:S(2)}) async-start(s32[32,1,2]{2,1,0:T(1,128)} %copy.99), calls=%async_computation | async-start | bytes 32768 | tf_op jit(solution)/shard_map/all_to_all | solution.py:109
  47.8 9.7 %copy-start.29 = (s32[4]{0:T(128)S(1)}, s32[4]{0:T(128)}, u32[]{:S(2)}) copy-start(s32[4]{0:T(128)} %param.18) | copy-start | bytes 52
  47.8 9.7 %copy-start.33 = (bf16[128,512]{1,0:T(8,128)(2,1)S(1)}, bf16[128,512]{1,0:T(8,128)(2,1)}, u32[]{:S(2)}) copy-start(bf16[128,512]{1,0:T(8,128)(2,1)} %param.17) | copy-start | bytes 393220
  47.8 10.0 %copy-start.35 = (bf16[128]{0:T(256)(128)(2,1)S(1)}, bf16[128]{0:T(256)(128)(2,1)}, u32[]{:S(2)}) copy-start(bf16[128]{0:T(256)(128)(2,1)} %param.14) | copy-start | bytes 772
  47.8 10.0 %copy-start.36 = (bf16[64]{0:T(256)(128)(2,1)S(1)}, bf16[64]{0:T(256)(128)(2,1)}, u32[]{:S(2)}) copy-start(bf16[64]{0:T(256)(128)(2,1)} %param.16) | copy-start | bytes 388
  47.8 10.0 %copy-start.32 = (s32[14,1]{0,1:T(1,128)S(1)}, s32[14,1]{0,1:T(1,128)}, u32[]{:S(2)}) copy-start(s32[14,1]{0,1:T(1,128)} %param.20) | copy-start | bytes 172
  47.8 10.1 %copy-start.31 = (s32[4,16]{1,0:T(4,128)S(1)}, s32[4,16]{1,0:T(4,128)}, u32[]{:S(2)}) copy-start(s32[4,16]{1,0:T(4,128)} %param.19) | copy-start | bytes 772
  47.8 119.3 %all-to-all-start.1 = ((bf16[32,2,128,512]{3,2,1,0:T(8,128)(2,1)}), bf16[32,2,128,512]{3,2,1,0:T(8,128)(2,1)}, u32[]{:S(2)}, u32[]{:S(2)}) async-start(bf16[32,2,128,512]{3,2,1,0:T(8,128)(2,1)} %broadcast_select_fusion), calls=%async_computation.1 | async-start | bytes 16777216 | tf_op jit(solution)/shard_map/all_to_all | solution.py:117
  58.4 114.5 %copy-start.27 = (pred[1792]{0:T(1024)(128)(4,1)}, pred[1792]{0:T(1024)(128)(4,1)S(1)}, u32[]{:S(2)}) copy-start(pred[1792]{0:T(1024)(128)(4,1)S(1)} %broadcast_bitcast_fusion) | copy-start | bytes 5380
  174.6 34.5 %collective-permute-start.1 = (bf16[1792,512]{1,0:T(8,128)(2,1)}, bf16[1792,512]{1,0:T(8,128)(2,1)}, u32[]{:S(2)}, u32[]{:S(2)}) collective-permute-start(bf16[1792,512]{1,0:T(8,128)(2,1)} %bitcast_select_fusion), channel_id=1, source_target_pairs={{0,32},{32,64},{64,96},{96,0},{1,33},{33,65},{65,97},{97,1},{2,34}... | collective-permute-start | bytes 5505032 | tf_op jit(solution)/shard_map/ppermute | solution.py:19
  229.3 26.1 %collective-permute-start.3 = (bf16[1792,512]{1,0:T(8,128)(2,1)}, bf16[1792,512]{1,0:T(8,128)(2,1)}, u32[]{:S(2)}, u32[]{:S(2)}) collective-permute-start(bf16[1792,512]{1,0:T(8,128)(2,1)} %collective-permute-done.1), channel_id=1, source_target_pairs={{0,32},{32,64},{64,96},{96,0},{1,33},{33,65},{65,97},{97,1},{2,34}... | collective-permute-start | bytes 5505032 | tf_op jit(solution)/shard_map/ppermute | solution.py:19
  239.4 77.4 %collective-permute-start = (f32[1792,512]{1,0:T(8,128)}, f32[1792,512]{1,0:T(8,128)}, u32[]{:S(2)}, u32[]{:S(2)}) collective-permute-start(f32[1792,512]{1,0:T(8,128)} %copy.107), channel_id=1, source_target_pairs={{0,32},{32,64},{64,96},{96,0},{1,33},{33,65},{65,97},{97,1},{2,34}... | collective-permute-start | bytes 11010056 | tf_op jit(solution)/shard_map/ppermute | solution.py:19
  260.9 5.8 copy-start.3
  260.9 50.4 %collective-permute-start.5 = (bf16[1792,512]{1,0:T(8,128)(2,1)}, bf16[1792,512]{1,0:T(8,128)(2,1)}, u32[]{:S(2)}, u32[]{:S(2)}) collective-permute-start(bf16[1792,512]{1,0:T(8,128)(2,1)} %collective-permute-done.3), channel_id=1, source_target_pairs={{0,32},{32,64},{64,96},{96,0},{1,33},{33,65},{65,97},{97,1},{2,34}... | collective-permute-start | bytes 5505032 | tf_op jit(solution)/shard_map/ppermute | solution.py:19
  322.5 42.8 %collective-permute-start.2 = (f32[1792,512]{1,0:T(8,128)}, f32[1792,512]{1,0:T(8,128)}, u32[]{:S(2)}, u32[]{:S(2)}) collective-permute-start(f32[1792,512]{1,0:T(8,128)} %add.308), channel_id=1, source_target_pairs={{0,32},{32,64},{64,96},{96,0},{1,33},{33,65},{65,97},{97,1},{2,34}... | collective-permute-start | bytes 11010056 | tf_op jit(solution)/shard_map/ppermute | solution.py:19
  349.4 24.3 %copy-start.23 = (bf16[4,64,1792]{2,1,0:T(8,128)(2,1)S(1)}, bf16[4,64,1792]{2,1,0:T(8,128)(2,1)}, u32[]{:S(2)}) copy-start(bf16[4,64,1792]{2,1,0:T(8,128)(2,1)} %bitcast_convert_fusion) | copy-start | bytes 2752516
  371.2 42.6 %collective-permute-start.4 = (f32[1792,512]{1,0:T(8,128)}, f32[1792,512]{1,0:T(8,128)}, u32[]{:S(2)}, u32[]{:S(2)}) collective-permute-start(f32[1792,512]{1,0:T(8,128)} %add.319), channel_id=1, source_target_pairs={{0,32},{32,64},{64,96},{96,0},{1,33},{33,65},{65,97},{97,1},{2,34}... | collective-permute-start | bytes 11010056 | tf_op jit(solution)/shard_map/ppermute | solution.py:19
  417.7 22.9 %collective-permute-start.6 = (bf16[1792,512]{1,0:T(8,128)(2,1)S(1)}, bf16[1792,512]{1,0:T(8,128)(2,1)S(1)}, u32[]{:S(2)}, u32[]{:S(2)}) collective-permute-start(bf16[1792,512]{1,0:T(8,128)(2,1)S(1)} %add.330), channel_id=1, source_target_pairs={{0,32},{32,64},{64,96},{96,0},{1,33},{33,65},{65,97},{97,1},{2,34}... | collective-permute-start | bytes 5505032 | tf_op jit(solution)/shard_map/ppermute | solution.py:19
  450.0 131.5 %all-to-all-start.2 = ((bf16[32,2,128,512]{3,2,1,0:T(8,128)(2,1)}), bf16[32,2,128,512]{3,2,1,0:T(8,128)(2,1)}, u32[]{:S(2)}, u32[]{:S(2)}) async-start(bf16[32,2,128,512]{3,2,1,0:T(8,128)(2,1)} %bitcast.404), calls=%async_computation.2 | async-start | bytes 16777216 | tf_op jit(solution)/shard_map/all_to_all | solution.py:141
  458.0 346.1 %reduce-scatter.4.cloned.1.call-start = ((), (), s32[]{:S(2)}) async-start(), calls=%async_computation.5 | async-start | bytes 2162688
  608.6 10.8 %copy-start.2 = (f32[4096,512]{1,0:T(8,128)S(1)}, f32[4096,512]{1,0:T(8,128)}, u32[]{:S(2)}) copy-start(f32[4096,512]{1,0:T(8,128)} %reshape.288) | copy-start | bytes 25165828
  628.4 232.8 %all-reduce.2.cloned.1.call-start = ((), (), s32[]{:S(2)}) async-start(), calls=%async_computation.4 | async-start | bytes 524288 | tf_op jit(solution)/shard_map/psum | solution.py:155
  639.5 223.3 %copy-start.1 = (bf16[1024,512]{1,0:T(8,128)(2,1)S(1)}, bf16[1024,512]{1,0:T(8,128)(2,1)}, u32[]{:S(2)}) copy-start(bf16[1024,512]{1,0:T(8,128)(2,1)} %param.12) | copy-start | bytes 3145732
  (25 other events, 56.0 us)
Sparse Core Ops, SparseCore 0:
  628.5 175.5 reduce-scatter.3
  806.8 54.3 all-reduce.1
where the time goes:
time: 877 us; the launch traced here: 870 us
  waiting for transfers between devices  552 us (63%)
  local copies, waits for them, and re-layouts  103 us (12%)
  matrix products  102 us (12%)
  starting transfers between devices  53.8 us (6%)
  other arithmetic  43.6 us (5%)
  between operations  15 us (2%)
    unnamed x3, waiting for transfers between devices  163 us
    all_to_all x1, waiting for transfers between devices, shards(): lax.all_to_all(returning.reshape(owner_count, CAP, BLK, E), 'shard', spli...  123 us
    all_to_all x1, waiting for transfers between devices, shards(): lax.all_to_all(outgoing, 'shard', split_axis=0, concat_axis=0, tiled=True)  109 us
    ppermute x7, waiting for transfers between devices, from_behind(): return lax.ppermute(x, axis, [(i, (i + by) % peers) for i in range(peers)])  103 us
    psum x1, waiting for transfers between devices, shards(): tower_gradient = lax.psum(tower_part, 'blk')  54.4 us
    unnamed x78, local copies, waits for them, and re-layouts  27 us
    ppermute x7, starting transfers between devices, from_behind(): return lax.ppermute(x, axis, [(i, (i + by) % peers) for i in range(peers)])  24.5 us
    dot_general x4, matrix products, pair_terms(): jnp.einsum('pg,ugi->upi', gate_in, hidden_grad, preferred_element_type=jn...  21.7 us
  transfers between devices with their start and end apart: 12, of which 9 were waited for; matrix products, arithmetic and copies ran while one was open for 14% of the time, Pallas kernels for 0%

commit v1 on v0

--- a/solution.py
+++ b/solution.py
@@ -1,3 +1,4 @@
+import functools
 import math
 import jax
 import jax.numpy as jnp
@@ -12,6 +13,13 @@
 USERS = 4
 UTAB = 128
 E = 512
+
+
+def _trace_stocks(load, device_axis):
+    return jnp.sum(lax.all_gather(load, axis_name=device_axis), axis=0)
+
+
+unite_the_table = functools.partial(_trace_stocks, device_axis="blk")
 
 
 def from_behind(x, axis, by):
@@ -152,7 +160,7 @@
     summed = jnp.dot(slot_hot, returned, preferred_element_type=jnp.float32).reshape(OWN * BLK, E)
     partial_value = split_product(item_features, summed)
     tower_part = lax.psum_scatter(partial_value, "shard", scatter_dimension=0, tiled=True)
-    tower_gradient = lax.psum(tower_part, "blk")
+    tower_gradient = unite_the_table(tower_part)
     user_gradient = split_product(row_match.astype(jnp.bfloat16), user_delta)
     return (tower_gradient, user_gradient)
 

time: 877 us -> 849 us (0.968)
  waiting for transfers between devices: 552 us -> 496 us
  blocking collectives: 0 us -> 30.6 us
    unnamed x3 -> x1, waiting for transfers between devices: 163 us -> 0.02 us
    reduce_scatter x0 -> x1, waiting for transfers between devices: none -> 161 us  [shards(): lax.psum_scatter(partial_value, 'shard', scatter_dimension=0, tiled=True)]
    psum x1 -> x0, waiting for transfers between devices: 54.4 us -> none  [shards(): tower_gradient = lax.psum(tower_part, 'blk')]
    all_gather x0 -> x1, blocking collectives: none -> 30.6 us  [_trace_stocks(): return jnp.sum(lax.all_gather(load, axis_name=device_axis), axis=0)]
    unnamed x78 -> x76, local copies, waits for them, and re-layouts: 27 us -> 24 us
  transfers between devices with their start and end apart: 12 -> 11, of which waited for: 9 -> 8; matrix products, arithmetic and copies ran while one was open for 14% -> 14% of each run, Pallas kernels for 0% -> 0%
where the time goes in v1:
time: 849 us; the launch traced here: 842 us
  waiting for transfers between devices  496 us (58%)
  matrix products  102 us (12%)
  local copies, waits for them, and re-layouts  100 us (12%)
  starting transfers between devices  53.5 us (6%)
  other arithmetic  44.3 us (5%)
  blocking collectives  30.6 us (4%)
  between operations  15 us (2%)
    reduce_scatter x1, waiting for transfers between devices, shards(): lax.psum_scatter(partial_value, 'shard', scatter_dimension=0, tiled=True)  161 us
    all_to_all x1, waiting for transfers between devices, shards(): lax.all_to_all(returning.reshape(owner_count, CAP, BLK, E), 'shard', spli...  123 us
    all_to_all x1, waiting for transfers between devices, shards(): lax.all_to_all(outgoing, 'shard', split_axis=0, concat_axis=0, tiled=True)  109 us
    ppermute x7, waiting for transfers between devices, from_behind(): return lax.ppermute(x, axis, [(i, (i + by) % peers) for i in range(peers)])  103 us
    all_gather x1, blocking collectives, _trace_stocks(): return jnp.sum(lax.all_gather(load, axis_name=device_axis), axis=0)  30.6 us
    ppermute x7, starting transfers between devices, from_behind(): return lax.ppermute(x, axis, [(i, (i + by) % peers) for i in range(peers)])  24.5 us
    unnamed x76, local copies, waits for them, and re-layouts  24 us
    dot_general x4, matrix products, pair_terms(): jnp.einsum('pg,ugi->upi', gate_in, hidden_grad, preferred_element_type=jn...  21.7 us
  transfers between devices with their start and end apart: 11, of which 8 were waited for; matrix products, arithmetic and copies ran while one was open for 14% of the time, Pallas kernels for 0%

profile of v1, /device:TPU:1, one launch (start us, length us, event | category | flops | bytes accessed | tf_op | source)
XLA Modules:
  0.0 841.7 jit_solution(1913135747654138640)
XLA Ops:
  10.4 11.3 %all-to-all-start = ((s32[32,1,2]{2,1,0:T(1,128)}), s32[32,1,2]{2,1,0:T(1,128)S(1)}, u32[]{:S(2)}, u32[]{:S(2)}) async-start(s32[32,1,2]{2,1,0:T(1,128)} %copy.98), calls=%async_computation | async-start | bytes 32768 | tf_op jit(solution)/shard_map/all_to_all | solution.py:117
  21.8 9.5 %convolution_convert_fusion = bf16[4096,512]{1,0:T(8,128)(2,1)} fusion(bf16[4096,1024]{1,0:T(8,128)(2,1)} %param.11, bf16[1024,512]{1,0:T(8,128)(2,1)S(1)} %copy-done), kind=kOutput, calls=%fused_computation.9 | convolution fusion | flops 4297064448 | bytes 13631488 | tf_op jit(solution)/shard_map/dot_general | solution.py:120
  32.8 7.5 gather_fusion
  40.3 7.5 broadcast_select_fusion
  47.8 9.6 %all-to-all-start.1 = ((bf16[32,2,128,512]{3,2,1,0:T(8,128)(2,1)}), bf16[32,2,128,512]{3,2,1,0:T(8,128)(2,1)}, u32[]{:S(2)}, u32[]{:S(2)}) async-start(bf16[32,2,128,512]{3,2,1,0:T(8,128)(2,1)} %broadcast_select_fusion), calls=%async_computation.1 | async-start | bytes 16777216 | tf_op jit(solution)/shard_map/all_to_all | solution.py:125
  58.5 108.7 %all-to-all-done.1 = bf16[32,2,128,512]{3,2,1,0:T(8,128)(2,1)} async-done(((bf16[32,2,128,512]{3,2,1,0:T(8,128)(2,1)}), bf16[32,2,128,512]{3,2,1,0:T(8,128)(2,1)}, u32[]{:S(2)}, u32[]{:S(2)}) %all-to-all-start.1) | async-done | bytes 8388640 | tf_op jit(solution)/shard_map/all_to_all | solution.py:125
  174.6 14.0 %collective-permute-start.1 = (bf16[1792,512]{1,0:T(8,128)(2,1)}, bf16[1792,512]{1,0:T(8,128)(2,1)}, u32[]{:S(2)}, u32[]{:S(2)}) collective-permute-start(bf16[1792,512]{1,0:T(8,128)(2,1)} %bitcast_select_fusion), channel_id=1, source_target_pairs={{0,32},{32,64},{64,96},{96,0},{1,33},{33,65},{65,97},{97,1},{2,34}... | collective-permute-start | bytes 5505032 | tf_op jit(solution)/shard_map/ppermute | solution.py:27
  249.9 5.5 copy.112
  271.1 40.1 %collective-permute-done.5 = bf16[1792,512]{1,0:T(8,128)(2,1)} collective-permute-done((bf16[1792,512]{1,0:T(8,128)(2,1)}, bf16[1792,512]{1,0:T(8,128)(2,1)}, u32[]{:S(2)}, u32[]{:S(2)}) %collective-permute-start.5) | collective-permute-done | bytes 1835040 | tf_op jit(solution)/shard_map/ppermute | solution.py:27
  334.5 6.1 fusion.55
  349.5 15.8 %collective-permute-done.2 = f32[1792,512]{1,0:T(8,128)} collective-permute-done((f32[1792,512]{1,0:T(8,128)}, f32[1792,512]{1,0:T(8,128)}, u32[]{:S(2)}, u32[]{:S(2)}) %collective-permute-start.2) | collective-permute-done | bytes 3670048 | tf_op jit(solution)/shard_map/ppermute | solution.py:27
  365.3 5.9 add.317
  390.5 23.4 %collective-permute-done.4 = f32[1792,512]{1,0:T(8,128)} collective-permute-done((f32[1792,512]{1,0:T(8,128)}, f32[1792,512]{1,0:T(8,128)}, u32[]{:S(2)}, u32[]{:S(2)}) %collective-permute-start.4) | collective-permute-done | bytes 3670048 | tf_op jit(solution)/shard_map/ppermute | solution.py:27
  420.4 20.2 %collective-permute-done.6 = bf16[1792,512]{1,0:T(8,128)(2,1)S(1)} collective-permute-done((bf16[1792,512]{1,0:T(8,128)(2,1)S(1)}, bf16[1792,512]{1,0:T(8,128)(2,1)S(1)}, u32[]{:S(2)}, u32[]{:S(2)}) %collective-permute-start.6) | collective-permute-done | bytes 1835040 | tf_op jit(solution)/shard_map/ppermute | solution.py:27
  444.9 5.2 scatter_fusion
  450.1 8.0 all-to-all-start.2
  458.2 123.1 %all-to-all-done.2 = bf16[32,2,128,512]{3,2,1,0:T(8,128)(2,1)} async-done(((bf16[32,2,128,512]{3,2,1,0:T(8,128)(2,1)}), bf16[32,2,128,512]{3,2,1,0:T(8,128)(2,1)}, u32[]{:S(2)}, u32[]{:S(2)}) %all-to-all-start.2) | async-done | bytes 8388640 | tf_op jit(solution)/shard_map/all_to_all | solution.py:149
  581.3 11.8 %copy.141 = bf16[8,8,128,512]{3,1,2,0:T(8,128)(2,1)} copy(bf16[8,8,128,512]{3,2,1,0:T(8,128)(2,1)} %bitcast.68) | data formatting | bytes 16777216
  593.0 7.8 fusion.121
  600.9 7.7 reshape.288
  608.6 10.8 %fusion.4 = f32[512,1024]{1,0:T(8,128)S(1)} fusion(bf16[4096,1024]{1,0:T(8,128)(2,1)} %param.11, f32[4096,512]{1,0:T(8,128)} %reshape.288), kind=kOutput, calls=%fused_computation.10 | convolution fusion | flops 4303355904 | bytes 18874368 | tf_op jit(solution)/shard_map/dot_general | solution.py:86
  619.3 7.1 add_bitcast_fusion
  642.3 161.0 %reduce-scatter.4.cloned.1.call-done = f32[32,512]{1,0:T(8,128)} async-done(((f32[1024,512]{1,0:T(8,128)}), f32[32,512]{1,0:T(8,128)}) %reduce-scatter.4.cloned.1.call-update) | async-done | bytes 65552 | tf_op jit(solution)/shard_map/reduce_scatter | solution.py:162
  803.3 30.6 %all-gather = f32[128,512]{1,0:T(8,128)S(1)} all-gather(f32[32,512]{1,0:T(8,128)} %reduce-scatter.4.cloned.1.call-done), channel_id=2, replica_groups=mesh['blk'=4,'shard'=32] {'blk'}, dimensions={0}, use_global_device_ids=true | all-gather | bytes 327680 | tf_op jit(solution)/shard_map/all_gather | solution.py:19
  (176 shorter events, 168.5 us)
Async XLA Ops:
  7.2 14.6 %copy-start = (bf16[1024,512]{1,0:T(8,128)(2,1)S(1)}, bf16[1024,512]{1,0:T(8,128)(2,1)}, u32[]{:S(2)}) copy-start(bf16[1024,512]{1,0:T(8,128)(2,1)} %param.12) | copy-start | bytes 3145732
  10.4 20.8 %all-to-all-start = ((s32[32,1,2]{2,1,0:T(1,128)}), s32[32,1,2]{2,1,0:T(1,128)S(1)}, u32[]{:S(2)}, u32[]{:S(2)}) async-start(s32[32,1,2]{2,1,0:T(1,128)} %copy.98), calls=%async_computation | async-start | bytes 32768 | tf_op jit(solution)/shard_map/all_to_all | solution.py:117
  47.8 9.7 %copy-start.29 = (s32[4]{0:T(128)S(1)}, s32[4]{0:T(128)}, u32[]{:S(2)}) copy-start(s32[4]{0:T(128)} %param.18) | copy-start | bytes 52
  47.8 9.7 %copy-start.33 = (bf16[128,512]{1,0:T(8,128)(2,1)S(1)}, bf16[128,512]{1,0:T(8,128)(2,1)}, u32[]{:S(2)}) copy-start(bf16[128,512]{1,0:T(8,128)(2,1)} %param.17) | copy-start | bytes 393220
  47.8 10.0 %copy-start.35 = (bf16[128]{0:T(256)(128)(2,1)S(1)}, bf16[128]{0:T(256)(128)(2,1)}, u32[]{:S(2)}) copy-start(bf16[128]{0:T(256)(128)(2,1)} %param.14) | copy-start | bytes 772
  47.8 10.0 %copy-start.36 = (bf16[64]{0:T(256)(128)(2,1)S(1)}, bf16[64]{0:T(256)(128)(2,1)}, u32[]{:S(2)}) copy-start(bf16[64]{0:T(256)(128)(2,1)} %param.16) | copy-start | bytes 388
  47.8 10.0 %copy-start.32 = (s32[14,1]{0,1:T(1,128)S(1)}, s32[14,1]{0,1:T(1,128)}, u32[]{:S(2)}) copy-start(s32[14,1]{0,1:T(1,128)} %param.20) | copy-start | bytes 172
  47.8 10.1 %copy-start.31 = (s32[4,16]{1,0:T(4,128)S(1)}, s32[4,16]{1,0:T(4,128)}, u32[]{:S(2)}) copy-start(s32[4,16]{1,0:T(4,128)} %param.19) | copy-start | bytes 772
  47.8 119.3 %all-to-all-start.1 = ((bf16[32,2,128,512]{3,2,1,0:T(8,128)(2,1)}), bf16[32,2,128,512]{3,2,1,0:T(8,128)(2,1)}, u32[]{:S(2)}, u32[]{:S(2)}) async-start(bf16[32,2,128,512]{3,2,1,0:T(8,128)(2,1)} %broadcast_select_fusion), calls=%async_computation.1 | async-start | bytes 16777216 | tf_op jit(solution)/shard_map/all_to_all | solution.py:125
  58.5 114.5 %copy-start.27 = (pred[1792]{0:T(1024)(128)(4,1)}, pred[1792]{0:T(1024)(128)(4,1)S(1)}, u32[]{:S(2)}) copy-start(pred[1792]{0:T(1024)(128)(4,1)S(1)} %broadcast_bitcast_fusion) | copy-start | bytes 5380
  174.6 34.5 %collective-permute-start.1 = (bf16[1792,512]{1,0:T(8,128)(2,1)}, bf16[1792,512]{1,0:T(8,128)(2,1)}, u32[]{:S(2)}, u32[]{:S(2)}) collective-permute-start(bf16[1792,512]{1,0:T(8,128)(2,1)} %bitcast_select_fusion), channel_id=1, source_target_pairs={{0,32},{32,64},{64,96},{96,0},{1,33},{33,65},{65,97},{97,1},{2,34}... | collective-permute-start | bytes 5505032 | tf_op jit(solution)/shard_map/ppermute | solution.py:27
  229.3 26.1 %collective-permute-start.3 = (bf16[1792,512]{1,0:T(8,128)(2,1)}, bf16[1792,512]{1,0:T(8,128)(2,1)}, u32[]{:S(2)}, u32[]{:S(2)}) collective-permute-start(bf16[1792,512]{1,0:T(8,128)(2,1)} %collective-permute-done.1), channel_id=1, source_target_pairs={{0,32},{32,64},{64,96},{96,0},{1,33},{33,65},{65,97},{97,1},{2,34}... | collective-permute-start | bytes 5505032 | tf_op jit(solution)/shard_map/ppermute | solution.py:27
  239.4 77.4 %collective-permute-start = (f32[1792,512]{1,0:T(8,128)}, f32[1792,512]{1,0:T(8,128)}, u32[]{:S(2)}, u32[]{:S(2)}) collective-permute-start(f32[1792,512]{1,0:T(8,128)} %copy.106), channel_id=1, source_target_pairs={{0,32},{32,64},{64,96},{96,0},{1,33},{33,65},{65,97},{97,1},{2,34}... | collective-permute-start | bytes 11010056 | tf_op jit(solution)/shard_map/ppermute | solution.py:27
  260.9 5.8 copy-start.3
  260.9 50.4 %collective-permute-start.5 = (bf16[1792,512]{1,0:T(8,128)(2,1)}, bf16[1792,512]{1,0:T(8,128)(2,1)}, u32[]{:S(2)}, u32[]{:S(2)}) collective-permute-start(bf16[1792,512]{1,0:T(8,128)(2,1)} %collective-permute-done.3), channel_id=1, source_target_pairs={{0,32},{32,64},{64,96},{96,0},{1,33},{33,65},{65,97},{97,1},{2,34}... | collective-permute-start | bytes 5505032 | tf_op jit(solution)/shard_map/ppermute | solution.py:27
  322.5 42.8 %collective-permute-start.2 = (f32[1792,512]{1,0:T(8,128)}, f32[1792,512]{1,0:T(8,128)}, u32[]{:S(2)}, u32[]{:S(2)}) collective-permute-start(f32[1792,512]{1,0:T(8,128)} %add.306), channel_id=1, source_target_pairs={{0,32},{32,64},{64,96},{96,0},{1,33},{33,65},{65,97},{97,1},{2,34}... | collective-permute-start | bytes 11010056 | tf_op jit(solution)/shard_map/ppermute | solution.py:27
  349.5 24.3 %copy-start.23 = (bf16[4,64,1792]{2,1,0:T(8,128)(2,1)S(1)}, bf16[4,64,1792]{2,1,0:T(8,128)(2,1)}, u32[]{:S(2)}) copy-start(bf16[4,64,1792]{2,1,0:T(8,128)(2,1)} %bitcast_convert_fusion) | copy-start | bytes 2752516
  371.3 5.0 copy-start.16
  371.3 42.6 %collective-permute-start.4 = (f32[1792,512]{1,0:T(8,128)}, f32[1792,512]{1,0:T(8,128)}, u32[]{:S(2)}, u32[]{:S(2)}) collective-permute-start(f32[1792,512]{1,0:T(8,128)} %add.317), channel_id=1, source_target_pairs={{0,32},{32,64},{64,96},{96,0},{1,33},{33,65},{65,97},{97,1},{2,34}... | collective-permute-start | bytes 11010056 | tf_op jit(solution)/shard_map/ppermute | solution.py:27
  417.7 22.9 %collective-permute-start.6 = (bf16[1792,512]{1,0:T(8,128)(2,1)S(1)}, bf16[1792,512]{1,0:T(8,128)(2,1)S(1)}, u32[]{:S(2)}, u32[]{:S(2)}) collective-permute-start(bf16[1792,512]{1,0:T(8,128)(2,1)S(1)} %add.328), channel_id=1, source_target_pairs={{0,32},{32,64},{64,96},{96,0},{1,33},{33,65},{65,97},{97,1},{2,34}... | collective-permute-start | bytes 5505032 | tf_op jit(solution)/shard_map/ppermute | solution.py:27
  450.1 131.2 %all-to-all-start.2 = ((bf16[32,2,128,512]{3,2,1,0:T(8,128)(2,1)}), bf16[32,2,128,512]{3,2,1,0:T(8,128)(2,1)}, u32[]{:S(2)}, u32[]{:S(2)}) async-start(bf16[32,2,128,512]{3,2,1,0:T(8,128)(2,1)} %bitcast.405), calls=%async_computation.2 | async-start | bytes 16777216 | tf_op jit(solution)/shard_map/all_to_all | solution.py:149
  458.1 345.3 %reduce-scatter.4.cloned.1.call-start = ((), (), s32[]{:S(2)}) async-start(), calls=%async_computation.4 | async-start | bytes 2162688 | tf_op jit(solution)/shard_map/reduce_scatter | solution.py:162
  608.6 10.8 %copy-start.2 = (f32[4096,512]{1,0:T(8,128)S(1)}, f32[4096,512]{1,0:T(8,128)}, u32[]{:S(2)}) copy-start(f32[4096,512]{1,0:T(8,128)} %reshape.288) | copy-start | bytes 25165828
  639.5 195.1 %copy-start.1 = (bf16[1024,512]{1,0:T(8,128)(2,1)S(1)}, bf16[1024,512]{1,0:T(8,128)(2,1)}, u32[]{:S(2)}) copy-start(bf16[1024,512]{1,0:T(8,128)(2,1)} %param.12) | copy-start | bytes 3145732
  (24 other events, 50.9 us)
Sparse Core Ops, SparseCore 0:
  628.5 174.8 reduce-scatter.3
